TPU v7x, 32 devices: a whole 2x2x4 slice. The times are simulated.
32 devices in a mesh: pole: 4 (over y, x), blk: 8 (over z, core).
Axes of the slice: x: 2, y: 2, z: 4, core: 2. Of those that a mesh axis runs over, the one named last changes fastest.
Arguments:
- inverse_blocks: bfloat16 [8, 8192, 256], P('pole', 'blk'), may hold values from -6 to 6
- panel_blocks: bfloat16 [8, 1024, 1024], P('pole', 'blk'), may hold values from -0.125 to 0.125
- ancestor_mask: int32 [8, 4], P('blk'), may hold values 0 or 1
- diag_inverse: float32 [8, 512, 256], P('pole', 'blk'), may hold values from -6 to 6
- pole_weights: float32 [8, 2], replicated, may hold values from -6 to 6
- pole_order: int32 [8], replicated, may hold values from 0 to 7, each once
Outputs:
- density_columns: float32 [1024, 512], P('blk', 'pole')
- density_diag: float32 [512, 128], P('blk', 'pole')
Inputs may be any that keep to these rules, and one draw needn't show every extreme that they name: `pole_order`: each data position names a different pole number.
All inputs are finite; a program needn't handle non-finite values. No bound on the sum of `ancestor_mask` on one device may be relied on, other than what follows from the above.
Results may differ from a plain program's by a relative error of at most 0.0003.
Values may be sent and summed in bfloat16 or wider, within the bound.
A program may use at most 128 MiB of HBM per device.

v0:
```python
import jax
import jax.numpy as jnp
from jax import lax
from jax.sharding import PartitionSpec as P

PC = 8


def from_behind(array, axis, by):
    size = lax.axis_size(axis)
    return lax.ppermute(array, axis, [(i, (i + by) % size) for i in range(size)])


def from_partner(value, axis, stride):
    mask = 2**stride
    pairs = [(source, source ^ mask) for source in range(lax.axis_size(axis))]
    return lax.ppermute(value, axis, pairs)


def real_form(blocks):
    half_size = blocks.shape[-1] // 2
    lower_rows = jnp.concatenate([-blocks[..., half_size:], blocks[..., :half_size]], axis=-1)
    return jnp.concatenate([blocks, lower_rows], axis=-2)


def select_weights(pole_weights, pole_order, count):
    first_pole = lax.axis_index("pole") * count
    chosen = lax.dynamic_slice_in_dim(pole_order, first_pole, count, 0)
    numbers = jnp.arange(pole_weights.shape[0], dtype=jnp.int32)
    match_table = (chosen[:, None] == numbers[None, :]).astype(jnp.float32)
    return jnp.dot(match_table, pole_weights, precision=lax.Precision.HIGHEST)


def weighted_trace(left_blocks, right_blocks, weight_pairs, supernodes):
    width = left_blocks.shape[-1] // (2 * supernodes)
    shape = left_blocks.shape[:-1] + (2, supernodes, width)
    left_wide = left_blocks.astype(jnp.float32).reshape(shape)
    right_blocks = right_blocks.reshape(shape)
    right_real = right_blocks[..., 0, :, :]
    right_imag = right_blocks[..., 1, :, :]
    weight_real = weight_pairs[:, 0, None, None, None, None]
    weight_imag = weight_pairs[:, 1, None, None, None, None]
    combined = jnp.stack(
        [
            weight_real * right_real - weight_imag * right_imag,
            -weight_real * right_imag - weight_imag * right_real,
        ],
        axis=3,
    )
    total = jnp.einsum("pcutkx,pcutky->kxy", left_wide, combined, precision=lax.Precision.HIGHEST)
    return -total.reshape(supernodes * width, width)


def per_device(inverse_blocks, panel_blocks, ancestor_mask, diag_inverse, pole_weights, pole_order):
    pole_count = panel_blocks.shape[0]
    width = panel_blocks.shape[1]
    supernodes = ancestor_mask.shape[1]
    span = supernodes * width
    device_rank = lax.axis_index("blk")
    row_groups = lax.axis_size("blk") // PC
    group_bits = PC.bit_length() - 1
    weight_pairs = select_weights(pole_weights, pole_order, pole_count)
    mask_row = jnp.broadcast_to(
        ancestor_mask[0].astype(jnp.bfloat16)[None, :, None], (2, supernodes, width)
    ).reshape(2 * span)
    own_panel = panel_blocks * mask_row[None, None, :]
    pieces = [own_panel]
    for offset in range(1, row_groups):
        pieces.append(from_behind(own_panel, "blk", offset * PC))
    ordered = jnp.stack(pieces[::-1], axis=1)
    ordered = jnp.roll(ordered, device_rank // PC + 1, axis=1)
    stacked = real_form(ordered).reshape(pole_count, row_groups * 2 * width, 2 * span)
    partial_value = -jnp.einsum(
        "pmk,pkn->pmn", inverse_blocks, stacked, preferred_element_type=jnp.float32
    )
    partial_value = partial_value.reshape(pole_count, PC, width, 2 * span)
    mask_f = ancestor_mask[0].astype(jnp.float32)
    weighted = jnp.sum(
        weight_pairs[:, 0, None, None, None] * partial_value[..., :span]
        - weight_pairs[:, 1, None, None, None] * partial_value[..., span:],
        axis=0,
    )
    buffer = weighted
    for section_bit in range(group_bits - 1, -1, -1):
        half_size = buffer.shape[0] // 2
        lower_half = buffer[:half_size]
        upper_half = buffer[half_size:]
        mine_upper = device_rank >> section_bit & 1 == 1
        sending = jnp.where(mine_upper, lower_half, upper_half)
        keeping = jnp.where(mine_upper, upper_half, lower_half)
        buffer = keeping + from_partner(sending, "blk", section_bit)
    density_rows = buffer[0]
    row_blocks = own_panel[:, None]
    for bit_index in range(group_bits):
        partner_piece = from_partner(row_blocks, "blk", bit_index)
        upper_side = device_rank >> bit_index & 1 == 1
        row_blocks = jnp.where(
            upper_side,
            jnp.concatenate([partner_piece, row_blocks], axis=1),
            jnp.concatenate([row_blocks, partner_piece], axis=1),
        )
    diag_term = weighted_trace(row_blocks, partial_value, weight_pairs, supernodes)
    density_rows = (density_rows.reshape(width, supernodes, width) * mask_f[None, :, None]).reshape(
        width, span
    )
    diag_rows = lax.psum_scatter(diag_term, "blk", scatter_dimension=0, tiled=True)
    diag_rows = diag_rows + jnp.sum(
        weight_pairs[:, 0, None, None] * diag_inverse[..., :width]
        - weight_pairs[:, 1, None, None] * diag_inverse[..., width:],
        axis=0,
    )
    density_out, diag_out = (
        lax.psum_scatter(density_rows, "pole", scatter_dimension=1, tiled=True),
        lax.psum_scatter(diag_rows, "pole", scatter_dimension=1, tiled=True),
    )
    return (density_out, diag_out)


def solution(mesh):
    placed = (
        P("pole", "blk", None),
        P("pole", "blk", None),
        P("blk", None),
        P("pole", "blk", None),
        P(),
        P(),
    )
    return jax.shard_map(
        per_device,
        mesh=mesh,
        in_specs=placed,
        out_specs=(P("blk", "pole"), P("blk", "pole")),
        check_vma=False,
    )
```

profile of v0, /device:TPU:0, one launch (start us, length us, event | category | flops | bytes accessed | tf_op | source)
XLA Modules:
  0.0 281.4 jit_solution(3820896559708431049)
XLA Ops:
  7.2 0.8 convert_bitcast_fusion
  8.0 0.1 broadcast_in_dim.2
  8.1 1.1 fusion.32
  9.1 0.6 collective-permute-start.3
  9.7 0.7 dynamic_slice.5
  10.4 0.9 fusion.22
  11.3 0.2 slice_reduce_fusion.1
  11.5 1.1 maximum_select_fusion.8
  12.7 2.6 collective-permute-start.4
  15.3 1.3 convolution_negate_fusion
  16.6 1.3 fusion.5
  17.9 1.9 copy-done.1
  19.8 1.2 slice_select_fusion
  21.0 2.6 collective-permute-start
  23.6 10.6 %reshape_reshape.3 = f32[2,8,128,2,4,128]{5,4,3,2,1,0:T(4,128)} reshape(f32[2,1024,1024]{2,1,0:T(8,128)} %bitcast.42) | data formatting | bytes 16777216 | tf_op jit(solution)/shard_map/reshape;reshape | solution.py:38
  34.2 21.8 %collective-permute-done.4 = bf16[2,2,128,1024]{3,2,0,1:T(8,128)(2,1)} collective-permute-done((bf16[2,2,128,1024]{3,2,0,1:T(8,128)(2,1)}, bf16[2,2,128,1024]{3,2,0,1:T(8,128)(2,1)}, u32[]{:S(2)}, u32[]{:S(2)}) %collective-permute-start.4) | collective-permute-done | bytes 1048608 | tf_op jit(solution)/shard_map/ppermute | solution.py:17
  56.0 3.9 %maximum_select_fusion.2 = bf16[2,4,128,1024]{3,2,0,1:T(8,128)(2,1)} fusion(bf16[2,2,128,1024]{3,2,0,1:T(8,128)(2,1)} %maximum_select_fusion.8, bf16[2,2,128,1024]{3,2,0,1:T(8,128)(2,1)} %collective-permute-done.4, pred[]{:T(512)S(6)} %eq.29), kind=kLoop, calls=%fused_computation.18 | loop fusion | flops 3145728 | bytes 4194305 | tf_op jit(solution)/shard_map/jit(_where)/select_n | solution.py:97
  59.9 0.7 collective-permute-start.5
  60.7 4.0 %fusion.29 = (f32[2,8,128,1,4,128]{5,4,3,2,1,0:T(4,128)S(1)}, f32[2,8,128,1,4,128]{5,4,3,2,1,0:T(4,128)S(1)}) fusion(f32[2,8,128,2,4,128]{5,4,3,2,1,0:T(4,128)} %reshape_reshape.3), kind=kLoop, calls=%fused_computation.50 | loop fusion | bytes 16777216 | tf_op jit(solution)/shard_map/slice | solution.py:39
  64.7 4.8 %multiply_subtract_fusion.1 = (f32[2,8,128,1,4,128]{5,2,3,4,0,1:T(8,128)}, f32[2,8,128,1,4,128]{5,2,3,4,0,1:T(8,128)}) fusion(f32[2,8,128,1,4,128]{5,4,3,2,1,0:T(4,128)S(1)} %get-tuple-element.11, f32[2,8,128,1,4,128]{5,4,3,2,1,0:T(4,128)S(1)} %get-tuple-element.10, f32[2]{0:T(128)S(1)} %get-tuple-element.7, f32[2]{0:T(128)S(1)} %get-tuple-element.6, ...), kind=kLoop, calls=%fused_computation.15 | loop fusion | flops 6291456 | bytes 16777240 | tf_op jit(solution)/shard_map/sub | solution.py:45
  69.5 46.3 %collective-permute-done = f32[4,128,512]{2,1,0:T(8,128)} collective-permute-done((f32[4,128,512]{2,1,0:T(8,128)}, f32[4,128,512]{2,1,0:T(8,128)}, u32[]{:S(2)}, u32[]{:S(2)}) %collective-permute-start) | collective-permute-done | bytes 1048608 | tf_op jit(solution)/shard_map/ppermute | solution.py:17
  115.8 1.6 select_add_fusion
  117.3 1.0 copy-done.2
  118.3 0.9 slice_select_fusion.1
  119.2 0.4 concatenate.57
  119.6 0.4 copy.44
  120.0 1.4 concatenate.56
  121.4 0.4 copy.43
  121.8 0.2 maximum_select_fusion.9
  122.0 2.7 concatenate.55
  124.7 2.4 copy.47
  127.0 3.3 %maximum_select_fusion.3 = bf16[2,4,128,2,4,128]{2,5,3,4,0,1:T(8,128)(2,1)} fusion(bf16[2,2,128,2,4,128]{2,5,3,4,0,1:T(8,128)(2,1)S(1)} %maximum_select_fusion.9, bf16[2,2,128,2,4,128]{2,5,3,4,0,1:T(8,128)(2,1)} %copy.47, pred[]{:T(512)S(6)} %eq.29), kind=kLoop, calls=%fused_computation.19 | loop fusion | flops 3145728 | bytes 4194305 | tf_op jit(solution)/shard_map/jit(_where)/select_n | solution.py:97
  130.3 40.8 %collective-permute-done.1 = f32[2,128,512]{2,1,0:T(8,128)} collective-permute-done((f32[2,128,512]{2,1,0:T(8,128)}, f32[2,128,512]{2,1,0:T(8,128)}, u32[]{:S(2)}, u32[]{:S(2)}) %collective-permute-start.1) | collective-permute-done | bytes 524320 | tf_op jit(solution)/shard_map/ppermute | solution.py:17
  171.1 2.0 select_add_fusion.1
  173.1 3.2 %concatenate.54 = bf16[2,4,128,2,4,128]{5,4,3,2,0,1:T(4,128)(2,1)S(1)} reshape(bf16[2,4,128,1024]{3,2,0,1:T(8,128)(2,1)} %collective-permute-done.5) | data formatting | bytes 4194304 | tf_op jit(solution)/shard_map/concatenate | solution.py:99
  176.4 2.6 copy.49
  179.0 11.5 %fusion.15 = f32[4,128,128]{2,1,0:T(8,128)} fusion(f32[2,8,128,1,4,128]{5,2,3,4,0,1:T(8,128)} %get-tuple-element.9, f32[2,8,128,1,4,128]{5,2,3,4,0,1:T(8,128)} %get-tuple-element.8, bf16[2,4,128,2,4,128]{2,5,3,4,0,1:T(8,128)(2,1)} %maximum_select_fusion.3, bf16[2,4,128,2,4,128]{2,5,3,4,0,1:T(8,128)(2,1)} %copy.49, pred[]{:T(512)S(6)} %eq.30), kind=kOutput, calls=%fused_computation.21 | convolution fusion | flops 3229679616 | bytes 12845057 | tf_op jit(solution)/shard_map/pcutkx,pcutky->kxy/dot_general | solution.py:50
  190.5 0.0 reduce-scatter.8.cloned.1.call-start
  190.6 0.1 collective-permute-start.2
  190.7 0.1 broadcast_bitcast_fusion
  190.8 1.4 collective-permute-done.2
  192.2 0.8 bitcast_multiply_fusion
  193.1 0.1 subtract_reduce_fusion
  193.2 28.4 %reduce-scatter.10.cloned.1.call-done = f32[64,128]{1,0:T(8,128)} async-done(((f32[512,128]{1,0:T(8,128)}), f32[64,128]{1,0:T(8,128)}) %reduce-scatter.10.cloned.1.call-update) | async-done | bytes 32784 | tf_op jit(solution)/shard_map/reduce_scatter | solution.py:106
  221.6 0.8 add.33
  222.3 0.7 copy.59
  223.1 24.3 %reduce-scatter.8.cloned.1.call-done = f32[128,128]{1,0:T(8,128)} async-done(((f32[128,512]{1,0:T(8,128)}), f32[128,128]{1,0:T(8,128)}) %reduce-scatter.8.cloned.1.call-update) | async-done | bytes 65552 | tf_op jit(solution)/shard_map/reduce_scatter | solution.py:113
  247.4 27.4 %reduce-scatter.12.cloned.1.call-done = f32[32,64]{1,0:T(8,128)} async-done(((f32[128,64]{1,0:T(8,128)}), f32[32,64]{1,0:T(8,128)}) %reduce-scatter.12.cloned.1.call-update) | async-done | bytes 8208
  (26 shorter events, 0.3 us)
Async XLA Ops:
  7.2 8.2 %copy-start = (bf16[2,1024,256]{2,1,0:T(8,128)(2,1)S(1)}, bf16[2,1024,256]{2,1,0:T(8,128)(2,1)}, u32[]{:S(2)}) copy-start(bf16[2,1024,256]{2,1,0:T(8,128)(2,1)} %param.6) | copy-start | bytes 3145732
  7.2 214.4 %reduce-scatter.10.cloned.1.call-start = ((), (), s32[]{:S(2)}) async-start(), calls=%async_computation.4 | async-start | bytes 294912 | tf_op jit(solution)/shard_map/reduce_scatter | solution.py:106
  9.1 2.4 collective-permute-start.3
  11.5 5.1 %copy-start.5 = (bf16[2,1,128,1024]{3,2,0,1:T(8,128)(2,1)}, bf16[2,1,128,1024]{3,2,0,1:T(8,128)(2,1)S(1)}, u32[]{:S(2)}) copy-start(bf16[2,1,128,1024]{3,2,0,1:T(8,128)(2,1)S(1)} %collective-permute-done.3) | copy-start | bytes 1572868
  12.7 43.3 %collective-permute-start.4 = (bf16[2,2,128,1024]{3,2,0,1:T(8,128)(2,1)}, bf16[2,2,128,1024]{3,2,0,1:T(8,128)(2,1)}, u32[]{:S(2)}, u32[]{:S(2)}) collective-permute-start(bf16[2,2,128,1024]{3,2,0,1:T(8,128)(2,1)} %maximum_select_fusion.8), channel_id=1, source_target_pairs={{0,2},{1,3},{2,0},{3,1},{4,6},{5,7},{6,4},{7,5},{8,10},{9,11},{10,... | collective-permute-start | bytes 3145736 | tf_op jit(solution)/shard_map/ppermute | solution.py:17
  16.6 3.2 %copy-start.1 = (f32[2,1024,1024]{1,2,0:T(8,128)}, f32[2,1024,1024]{1,2,0:T(8,128)S(1)}, u32[]{:S(2)}) copy-start(f32[2,1024,1024]{1,2,0:T(8,128)S(1)} %convolution_negate_fusion) | copy-start | bytes 25165828
  21.0 94.7 %collective-permute-start = (f32[4,128,512]{2,1,0:T(8,128)}, f32[4,128,512]{2,1,0:T(8,128)}, u32[]{:S(2)}, u32[]{:S(2)}) collective-permute-start(f32[4,128,512]{2,1,0:T(8,128)} %slice_select_fusion), channel_id=1, source_target_pairs={{0,4},{1,5},{2,6},{3,7},{4,0},{5,1},{6,2},{7,3},{8,12},{9,13},{10,... | collective-permute-start | bytes 3145736 | tf_op jit(solution)/shard_map/ppermute | solution.py:17
  59.9 113.2 %collective-permute-start.5 = (bf16[2,4,128,1024]{3,2,0,1:T(8,128)(2,1)}, bf16[2,4,128,1024]{3,2,0,1:T(8,128)(2,1)}, u32[]{:S(2)}, u32[]{:S(2)}) collective-permute-start(bf16[2,4,128,1024]{3,2,0,1:T(8,128)(2,1)} %maximum_select_fusion.2), channel_id=1, source_target_pairs={{0,4},{1,5},{2,6},{3,7},{4,0},{5,1},{6,2},{7,3},{8,12},{9,13},{10,... | collective-permute-start | bytes 6291464 | tf_op jit(solution)/shard_map/ppermute | solution.py:17
  69.5 49.7 %copy-start.6 = (bf16[2,128,1024]{2,1,0:T(8,128)(2,1)S(1)}, bf16[2,128,1024]{2,1,0:T(8,128)(2,1)}, u32[]{:S(2)}) copy-start(bf16[2,128,1024]{2,1,0:T(8,128)(2,1)} %param.7) | copy-start | bytes 1572868
  117.3 1.0 copy-start.2
  119.2 51.9 %collective-permute-start.1 = (f32[2,128,512]{2,1,0:T(8,128)}, f32[2,128,512]{2,1,0:T(8,128)}, u32[]{:S(2)}, u32[]{:S(2)}) collective-permute-start(f32[2,128,512]{2,1,0:T(8,128)} %slice_select_fusion.1), channel_id=1, source_target_pairs={{0,2},{1,3},{2,0},{3,1},{4,6},{5,7},{6,4},{7,5},{8,10},{9,11},{10,... | collective-permute-start | bytes 1572872 | tf_op jit(solution)/shard_map/ppermute | solution.py:17
  122.0 49.2 %copy-start.3 = (f32[4,128,512]{2,1,0:T(8,128)S(1)}, f32[4,128,512]{2,1,0:T(8,128)}, u32[]{:S(2)}) copy-start(f32[4,128,512]{2,1,0:T(8,128)} %copy-done.2) | copy-start | bytes 3145732
  179.0 11.6 %copy-start.4 = (f32[2,128,512]{2,1,0:T(8,128)S(1)}, f32[2,128,512]{2,1,0:T(8,128)}, u32[]{:S(2)}) copy-start(f32[2,128,512]{2,1,0:T(8,128)} %select_add_fusion.1) | copy-start | bytes 1572868
  179.0 14.1 %copy-start.7 = (f32[2,64,256]{2,1,0:T(8,128)S(1)}, f32[2,64,256]{2,1,0:T(8,128)}, u32[]{:S(2)}) copy-start(f32[2,64,256]{2,1,0:T(8,128)} %param.9) | copy-start | bytes 393220
  190.5 56.9 %reduce-scatter.8.cloned.1.call-start = ((), (), s32[]{:S(2)}) async-start(), calls=%async_computation.3 | async-start | bytes 327680 | tf_op jit(solution)/shard_map/reduce_scatter | solution.py:113
  190.6 1.6 collective-permute-start.2
  193.0 81.8 %reduce-scatter.12.cloned.1.call-start = ((), (), s32[]{:S(2)}) async-start(), calls=%async_computation.5 | async-start | bytes 81920
Sparse Core Ops, SparseCore 0:
  190.6 30.8 reduce-scatter.9
  224.9 22.4 reduce-scatter.7
  250.7 24.0 reduce-scatter.11
where the time goes:
time: 282 us; the launch traced here: 281 us
  waiting for transfers between devices  191 us (68%)
  local copies, waits for them, and re-layouts  32.7 us (12%)
  other arithmetic  23.8 us (8%)
  between operations  13.9 us (5%)
  matrix products  13.6 us (5%)
  starting transfers between devices  6.71 us (2%)
    ppermute x6, waiting for transfers between devices, from_partner(): return lax.ppermute(value, axis, pairs)  110 us
    reduce_scatter x1, waiting for transfers between devices, per_device(): lax.psum_scatter(diag_term, 'blk', scatter_dimension=0, tiled=True)  28.4 us
    unnamed x4, waiting for transfers between devices  27.5 us
    reduce_scatter x1, waiting for transfers between devices, per_device(): lax.psum_scatter(density_rows, 'pole', scatter_dimension=1, tiled=True)  24.3 us
    concatenate x8, local copies, waits for them, and re-layouts, per_device(): jnp.concatenate([partner_piece, row_blocks], axis=1)  13.4 us
    dot_general x1, matrix products, weighted_trace(): jnp.einsum('pcutkx,pcutky->kxy', left_wide, combined, precision=lax.Preci...  11.5 us
    another operation x1, local copies, waits for them, and re-layouts, weighted_trace(): right_blocks = right_blocks.reshape(shape)  10.6 us
    select_n x4, other arithmetic, per_device(): jnp.where(upper_side, jnp.concatenate([partner_piece, row_blocks], axis=1...  8.52 us
  transfers between devices with their start and end apart: 9, of which 7 were waited for; matrix products, arithmetic and copies ran while one was open for 17% of the time, Pallas kernels for 0%

commit v1 on v0

v1 whole, which is shorter than its diff:
```python
import functools

import jax
import jax.numpy as jnp
from jax import lax
from jax.experimental import pallas as pl
from jax.experimental.pallas import tpu as pltpu
from jax.sharding import PartitionSpec as P

PC = 8
CHIPS = PC // 2
MESH = pl.DeviceIdType.MESH
F32 = jnp.float32
BF16 = jnp.bfloat16


def from_behind(array, axis, by):
    size = lax.axis_size(axis)
    return lax.ppermute(array, axis, [(i, (i + by) % size) for i in range(size)])


def dot00(left, right):
    return lax.dot_general(left, right, (((0,), (0,)), ((), ())), preferred_element_type=F32)


def kernel(cfg, *refs):
    n, rg, local, width, sn = cfg
    span = sn * width
    cw = span // n
    piece = span // (PC * rg)
    refs = list(refs)
    weight_ref, order_ref, mask_ref, inv_ref, own_ref = refs[:5]
    refs = refs[5:]
    col_ref = refs.pop(0) if rg > 1 else None
    diag_ref, dens_ref, dout_ref = refs[:3]
    (lall, gram, wfull, wrecv, wacc, wpole, wsum, wz, tbuf, trecv, tacc, tz, tsum, tpole,
     ss_z, ss_p, rs_z, rs_p, ss_wp, rs_wp, ss_wq, rs_wq, ss_wz, rs_wz,
     ss_tp, rs_tp, ss_tz, rs_tz, ss_tq, rs_tq) = refs[3:]

    me = lax.axis_index("blk")
    q = lax.axis_index("pole")
    rank = lax.rem(me, PC)
    first = me - rank
    z = rank // 2
    core = lax.rem(rank, 2)
    other = 1 - core

    def device(chip, which, pole):
        return {"pole": pole, "blk": first + 2 * chip + which}

    partner = device(z, other, q)

    def remote(src, dst, send, recv, where):
        return pltpu.make_async_remote_copy(
            src_ref=src, dst_ref=dst, send_sem=send, recv_sem=recv,
            device_id=where, device_id_type=MESH)

    peers = [partner]
    peers += [device(lax.rem(z + o, CHIPS), core, q) for o in range(1, CHIPS)]
    peers += [device(z, core, lax.rem(q + o, n)) for o in range(1, n)]
    barrier = pltpu.get_barrier_semaphore()
    for peer in peers:
        pl.semaphore_signal(barrier, inc=1, device_id=peer, device_id_type=MESH)
    pl.semaphore_wait(barrier, len(peers))

    def slot(p, chip, which):
        return lall.at[p, pl.ds(pl.multiple_of((2 * chip + which) * width, width), width)]

    def to_chip(src, p, chip, sgn, h):
        return remote(src, slot(p, chip, core), ss_z.at[(1 - sgn) // 2, h, p], rs_z.at[chip, p],
                      device(z + sgn, core, q))

    def to_partner(src, p, chip):
        return remote(src, slot(p, chip, core), ss_p.at[chip, p], rs_p.at[chip, p], partner)

    def inside(chip):
        return jnp.logical_and(chip >= 0, chip < CHIPS)

    for p in range(local):
        for sgn in (1, -1):
            @pl.when(inside(z + sgn))
            def _():
                to_chip(own_ref.at[p], p, z, sgn, 0).start()
    for p in range(local):
        to_partner(own_ref.at[p], p, z).start()

    poles = [order_ref[q * local + p] for p in range(local)]
    w_re = [weight_ref[poles[p], 0] for p in range(local)]
    w_im = [weight_ref[poles[p], 1] for p in range(local)]

    def column(p, a):
        return own_ref.at[p] if rg == 1 else col_ref.at[p, a]

    def part_copy(t):
        return remote(wfull.at[t, :, other], wrecv.at[t], ss_wp.at[t], rs_wp.at[t], partner)

    order = [lax.rem(q + o, n) for o in list(range(1, n)) + [0]]
    for t in order:
        total = None
        for p in range(local):
            product = None
            for a in range(rg):
                block = column(p, a)
                re = block[:, pl.ds(pl.multiple_of(t * cw, 128), cw)]
                im = block[:, pl.ds(pl.multiple_of(span + t * cw, 128), cw)]
                real_form = jnp.concatenate(
                    [jnp.concatenate([re, im], axis=1), jnp.concatenate([-im, re], axis=1)], axis=0)
                term = jnp.dot(inv_ref[p, :, 2 * width * a:2 * width * (a + 1)], real_form,
                               preferred_element_type=F32)
                product = term if product is None else product + term
            term = w_im[p] * product[:, cw:] - w_re[p] * product[:, :cw]
            total = term if total is None else total + term
        wfull[t] = total.reshape(CHIPS, 2, width, cw)
        part_copy(t).start()

    for p in range(local):
        lall[p, pl.ds(pl.multiple_of(rank * width, width), width)] = own_ref[p]

    def hop(h):
        for p in range(local):
            for sgn in (1, -1):
                chip = z - sgn * h

                @pl.when(inside(chip))
                def _():
                    here = slot(p, chip, core)
                    remote(here, here, ss_p.at[chip, p], rs_z.at[chip, p], partner).wait_recv()
                    if h < CHIPS - 1:
                        @pl.when(inside(z + sgn))
                        def _():
                            to_chip(here, p, chip, sgn, h).start()
                    to_partner(here, p, chip).start()

    def accumulate(chip, fresh):
        rows = pl.ds(pl.multiple_of(chip * 2 * width, 2 * width), 2 * width)
        for p in range(local):
            theirs = slot(p, chip, other)
            remote(theirs, theirs, ss_p.at[chip, p], rs_p.at[chip, p], partner).wait_recv()
            for a in range(rg):
                at = slice(2 * width * a, 2 * width * (a + 1))
                term = dot00(inv_ref[p, rows, at], lall[p, rows, :])
                gram[p, at, :] = term if fresh else gram[p, at, :] + term

    def gather(h):
        for sgn in (1, -1):
            chip = z - sgn * h

            @pl.when(inside(chip))
            def _():
                accumulate(chip, False)

    def pole_copy(o):
        to = lax.rem(q + o, n)
        return remote(wacc.at[to], wpole.at[o - 1], ss_wq.at[o - 1], rs_wq.at[o - 1], device(z, core, to))

    def line_copy(src, dst, send, recv, o):
        to = lax.rem(z + o, CHIPS)
        return remote(src.at[to], dst.at[o - 1], send.at[o - 1], recv.at[o - 1], device(to, core, q))

    hop(1)
    for o in list(range(1, n)) + [0]:
        t = lax.rem(q + o, n)
        part_copy(t).wait_recv()
        wacc[t] = wfull[t, :, core] + wrecv[t]
        if o:
            pole_copy(o).start()
    accumulate(z, True)
    gather(1)
    hop(2)
    for o in range(1, n):
        pole_copy(o).wait_recv()
    wsum[...] = wacc[q] + functools.reduce(lambda x, y: x + y, [wpole[o] for o in range(n - 1)])
    for o in range(1, CHIPS):
        line_copy(wsum, wz, ss_wz, rs_wz, o).start()
    gather(2)
    hop(3)
    gather(3)

    per_width = width // piece
    traces = [None] * sn
    for p in range(local):
        for a in range(rg):
            base = 2 * width * a
            upper = gram[p, base:base + width, :]
            lower = gram[p, base + width:base + 2 * width, :]
            m_re = upper[:, :span] - lower[:, span:]
            m_im = lower[:, :span] + upper[:, span:]
            n_re = w_re[p] * m_re - w_im[p] * m_im
            n_im = w_re[p] * m_im + w_im[p] * m_re
            both = jnp.concatenate([n_re, -n_im], axis=0)
            high = both.astype(BF16)
            low = (both - high.astype(F32)).astype(BF16)
            block = column(p, a)
            for k in range(sn):
                at = slice(k * width, (k + 1) * width)
                right = jnp.concatenate([block[:, at], block[:, span + k * width:span + (k + 1) * width]], axis=0)
                term = dot00(high[:, at], right) + dot00(low[:, at], right)
                traces[k] = term if traces[k] is None else traces[k] + term
    for g in range(PC * rg):
        k, off = g // per_width, g % per_width * piece
        tbuf[g % PC // 2, g % 2, g // PC] = traces[k][off:off + piece]
    trace_copy = remote(tbuf.at[:, other], trecv, ss_tp.at[0], rs_tp.at[0], partner)
    trace_copy.start()

    for o in range(1, CHIPS):
        line_copy(wsum, wz, ss_wz, rs_wz, o).wait_recv()
    rows = wsum[z] + functools.reduce(lambda x, y: x + y, [wz[o] for o in range(CHIPS - 1)])
    for j in range(cw // width):
        at = slice(j * width, (j + 1) * width)
        dens_ref[:, at] = rows[:, at] * mask_ref[0, q * (cw // width) + j].astype(F32)

    trace_copy.wait_recv()
    tacc[...] = tbuf[:, core] + trecv[...]
    for o in range(1, CHIPS):
        line_copy(tacc, tz, ss_tz, rs_tz, o).start()
    for o in range(1, CHIPS):
        line_copy(tacc, tz, ss_tz, rs_tz, o).wait_recv()
    summed = tacc[z] + functools.reduce(lambda x, y: x + y, [tz[o] for o in range(CHIPS - 1)])
    if rg > 1:
        dout_ref[...] = summed.reshape(rg * piece, width)
    else:
        summed = summed.reshape(piece, width)
        for p in range(local):
            summed = summed + w_re[p] * diag_ref[p, :, :width] - w_im[p] * diag_ref[p, :, width:]
        tsum[...] = summed

        def last_copy(o):
            return remote(tsum, tpole.at[o - 1], ss_tq.at[o - 1], rs_tq.at[o - 1],
                          device(z, core, lax.rem(q + o, n)))

        for o in range(1, n):
            last_copy(o).start()
        for o in range(1, n):
            last_copy(o).wait_recv()
        summed = summed + functools.reduce(lambda x, y: x + y, [tpole[o] for o in range(n - 1)])
        narrow = width // n
        result = jnp.zeros((piece, narrow), F32)
        for t in range(n):
            result = jnp.where(q == t, summed[:, t * narrow:(t + 1) * narrow], result)
        dout_ref[...] = result
        for o in range(1, n):
            last_copy(o).wait_send()

    for p in range(local):
        to_partner(own_ref.at[p], p, z).wait_send()
        for sgn in (1, -1):
            @pl.when(inside(z + sgn))
            def _():
                to_chip(own_ref.at[p], p, z, sgn, 0).wait_send()
            for h in range(1, CHIPS):
                chip = z - sgn * h

                @pl.when(inside(chip))
                def _():
                    here = slot(p, chip, core)
                    if h < CHIPS - 1:
                        @pl.when(inside(z + sgn))
                        def _():
                            to_chip(here, p, chip, sgn, h).wait_send()
                    to_partner(here, p, chip).wait_send()
    for t in range(n):
        part_copy(t).wait_send()
    for o in range(1, n):
        pole_copy(o).wait_send()
    trace_copy.wait_send()
    for o in range(1, CHIPS):
        line_copy(wsum, wz, ss_wz, rs_wz, o).wait_send()
        line_copy(tacc, tz, ss_tz, rs_tz, o).wait_send()


def per_device(inverse_blocks, panel_blocks, ancestor_mask, diag_inverse, pole_weights, pole_order):
    local, width = panel_blocks.shape[:2]
    sn = ancestor_mask.shape[1]
    span = sn * width
    n = lax.axis_size("pole")
    rg = lax.axis_size("blk") // PC
    cw = span // n
    piece = span // (PC * rg)
    me = lax.axis_index("blk")
    mask_row = jnp.broadcast_to(ancestor_mask[0].astype(BF16)[None, :, None], (2, sn, width)).reshape(2 * span)
    own_panel = panel_blocks * mask_row[None, None, :]
    arrays = [pole_weights, pole_order, ancestor_mask, inverse_blocks, own_panel]
    if rg > 1:
        pieces = [own_panel] + [from_behind(own_panel, "blk", o * PC) for o in range(1, rg)]
        arrays.append(jnp.roll(jnp.stack(pieces[::-1], axis=1), me // PC + 1, axis=1))
    arrays.append(diag_inverse)
    smem = pl.BlockSpec(memory_space=pltpu.SMEM)
    vmem = pl.BlockSpec(memory_space=pltpu.VMEM)
    diag_shape = (piece, width // n) if rg == 1 else (rg * piece, width)
    dma = pltpu.SemaphoreType.DMA
    density, diag = pl.pallas_call(
        functools.partial(kernel, (n, rg, local, width, sn)),
        out_shape=(jax.ShapeDtypeStruct((width, cw), F32), jax.ShapeDtypeStruct(diag_shape, F32)),
        in_specs=[smem] * 3 + [vmem] * (len(arrays) - 3),
        out_specs=(vmem, vmem),
        scratch_shapes=[
            pltpu.VMEM((local, PC * width, 2 * span), BF16),
            pltpu.VMEM((local, rg * 2 * width, 2 * span), F32),
            pltpu.VMEM((n, CHIPS, 2, width, cw), F32),
            pltpu.VMEM((n, CHIPS, width, cw), F32),
            pltpu.VMEM((n, CHIPS, width, cw), F32),
            pltpu.VMEM((n - 1, CHIPS, width, cw), F32),
            pltpu.VMEM((CHIPS, width, cw), F32),
            pltpu.VMEM((CHIPS - 1, width, cw), F32),
            pltpu.VMEM((CHIPS, 2, rg, piece, width), F32),
            pltpu.VMEM((CHIPS, rg, piece, width), F32),
            pltpu.VMEM((CHIPS, rg, piece, width), F32),
            pltpu.VMEM((CHIPS - 1, rg, piece, width), F32),
            pltpu.VMEM((piece, width), F32),
            pltpu.VMEM((n - 1, piece, width), F32),
            dma((2, CHIPS - 1, local)), dma((CHIPS, local)), dma((CHIPS, local)), dma((CHIPS, local)),
            dma((n,)), dma((n,)), dma((n - 1,)), dma((n - 1,)), dma((CHIPS - 1,)), dma((CHIPS - 1,)),
            dma((1,)), dma((1,)), dma((CHIPS - 1,)), dma((CHIPS - 1,)), dma((n - 1,)), dma((n - 1,)),
        ],
        compiler_params=pltpu.CompilerParams(collective_id=0, has_side_effects=True),
    )(*arrays)
    if rg > 1:
        groups = [[r * PC + b for r in range(rg)] for b in range(PC)]
        diag = lax.psum_scatter(diag, "blk", scatter_dimension=0, axis_index_groups=groups, tiled=True)
        chosen = lax.dynamic_slice_in_dim(pole_order, lax.axis_index("pole") * local, local, 0)
        pairs = pole_weights[chosen]
        diag = diag + jnp.sum(
            pairs[:, 0, None, None] * diag_inverse[..., :width] - pairs[:, 1, None, None] * diag_inverse[..., width:],
            axis=0)
        diag = lax.psum_scatter(diag, "pole", scatter_dimension=1, tiled=True)
    return density, diag


def solution(mesh):
    placed = (
        P("pole", "blk", None),
        P("pole", "blk", None),
        P("blk", None),
        P("pole", "blk", None),
        P(),
        P(),
    )
    return jax.shard_map(
        per_device,
        mesh=mesh,
        in_specs=placed,
        out_specs=(P("blk", "pole"), P("blk", "pole")),
        check_vma=False,
    )
```

time: 282 us -> 66.2 us (0.23)
  waiting for transfers between devices: 191 us -> 0 us
  Pallas kernels: 0 us -> 58.4 us
  local copies, waits for them, and re-layouts: 32.7 us -> 4.33 us
  other arithmetic: 23.8 us -> 2.52 us
  matrix products: 13.6 us -> 0 us
  between operations: 13.9 us -> 0.64 us
  starting transfers between devices: 6.71 us -> 0 us
    ppermute x6 -> x0, waiting for transfers between devices: 110 us -> none  [from_partner(): return lax.ppermute(value, axis, pairs)]
    pallas_call x0 -> x1, Pallas kernels: none -> 58.4 us  [per_device(): pl.pallas_call(functools.partial(kernel, (n, rg, local, width, sn)), out_...]
    reduce_scatter x2 -> x0, waiting for transfers between devices: 52.7 us -> none  [the longest x1 28.4 us: per_device(): lax.psum_scatter(diag_term, 'blk', scatter_dimension=0, tiled=True)]
    unnamed x4 -> x0, waiting for transfers between devices: 27.5 us -> none
    dot_general x3 -> x0, matrix products: 13.6 us -> none  [the longest x1 11.5 us: weighted_trace(): jnp.einsum('pcutkx,pcutky->kxy', left_wide, combined, precision=lax.Preci...]
    concatenate x8 -> x0, local copies, waits for them, and re-layouts: 13.4 us -> none  [per_device(): jnp.concatenate([partner_piece, row_blocks], axis=1)]
    select_n x7 -> x0, other arithmetic: 10.7 us -> none  [the longest x4 8.52 us: per_device(): jnp.where(upper_side, jnp.concatenate([partner_piece, row_blocks], axis=1...]
    another operation x1 -> x0, local copies, waits for them, and re-layouts: 10.6 us -> none  [weighted_trace(): right_blocks = right_blocks.reshape(shape)]
  transfers between devices with their start and end apart: 9 -> 0, of which waited for: 7 -> 0; matrix products, arithmetic and copies ran while one was open for 17% -> 0% of each run, Pallas kernels for 0% -> 0%
where the time goes in v1:
time: 66.2 us; the launch traced here: 65.9 us
  Pallas kernels  58.4 us (88%)
  local copies, waits for them, and re-layouts  4.33 us (7%)
  other arithmetic  2.52 us (4%)
    pallas_call x1, Pallas kernels, per_device(): pl.pallas_call(functools.partial(kernel, (n, rg, local, width, sn)), out_...  58.4 us
    unnamed x4, local copies, waits for them, and re-layouts  2.82 us
    mul x1, other arithmetic, per_device(): own_panel = panel_blocks * mask_row[None, None, :]  1.86 us
    pallas_call x1, local copies, waits for them, and re-layouts, per_device(): pl.pallas_call(functools.partial(kernel, (n, rg, local, width, sn)), out_...  1.44 us

profile of v1, /device:TPU:0, one launch (start us, length us, event | category | flops | bytes accessed | tf_op | source)
XLA Modules:
  0.0 65.9 jit_solution(12936966013417251856)
XLA Ops:
  0.6 0.7 %convert_bitcast_fusion = bf16[4]{0:T(256)(128)(2,1)S(1)} fusion(s32[1,4]{1,0:T(1,128)} %refs_2_.1), kind=kLoop, calls=%fused_computation.1 | loop fusion | flops 4 | bytes 24 | tf_op jit(solution)/shard_map/convert_element_type | solution.py:280
  1.3 0.1 broadcast_in_dim.2
  1.4 0.0 copy-start
  1.4 0.7 %copy-done = f32[8,2]{0,1:T(2,128)S(1)} copy-done((f32[8,2]{0,1:T(2,128)S(1)}, f32[8,2]{0,1:T(2,128)}, u32[]{:S(2)}) %copy-start) | copy-done | bytes 88
  2.0 0.7 %copy.8.refs_0_ = f32[8,2]{1,0:T(8,128)} copy(f32[8,2]{0,1:T(2,128)S(1)} %copy-done) | data formatting | bytes 128 | tf_op args[4]
  2.7 1.9 %broadcast_multiply_fusion.refs_4_ = bf16[2,128,1024]{2,1,0:T(8,128)(2,1)} fusion(bf16[2,128,1024]{2,1,0:T(8,128)(2,1)} %param.7, bf16[1024]{0:T(1024)(128)(2,1)S(1)} %bitcast.3), kind=kLoop, calls=%fused_computation | loop fusion | flops 262144 | bytes 1050624 | tf_op jit(solution)/shard_map/mul | solution.py:281
  4.6 58.4 %shard_map.77 = (f32[128,128]{1,0:T(8,128)}, f32[64,32]{1,0:T(8,128)}) custom-call(f32[8,2]{1,0:T(8,128)} %copy.8.refs_0_, s32[8]{0:T(128)} %refs_1_.1, s32[1,4]{1,0:T(1,128)} %refs_2_.1, bf16[2,1024,256]{2,1,0:T(8,128)(2,1)} %refs_3_.1, bf16[2,128,1024]{2,1,0:T(8,128)(2,1)} %broadcast_multiply_fusion.refs_4_, f32[2,64,256]{2,1,0:T(8,128)} %refs_5_.1), custom_call_target="tpu_custom_call" | custom-call | tf_op jit(solution)/shard_map/pallas_call | solution.py:291
  63.0 1.4 %copy.9 = f32[64,32]{0,1:T(8,128)} copy(f32[64,32]{1,0:T(8,128)} %get-tuple-element.3) | data formatting | bytes 16384 | tf_op jit(solution)/shard_map/pallas_call | solution.py:291
  64.4 1.5 %copy.11 = f32[128,128]{1,0:T(8,128)} copy(f32[128,128]{1,0:T(8,128)} %get-tuple-element.6) | data formatting | bytes 131072
Async XLA Ops:
  1.4 0.7 %copy-start = (f32[8,2]{0,1:T(2,128)S(1)}, f32[8,2]{0,1:T(2,128)}, u32[]{:S(2)}) copy-start(f32[8,2]{0,1:T(2,128)} %param.10) | copy-start | bytes 196

commit v2 on v1

--- a/solution.py
+++ b/solution.py
@@ -28,12 +28,14 @@
     span = sn * width
     cw = span // n
     piece = span // (PC * rg)
+    lean = rg == 1
+    half = CHIPS // 2
     refs = list(refs)
-    weight_ref, order_ref, mask_ref, inv_ref, own_ref = refs[:5]
+    weight_ref, order_ref, mask_ref, inv_hbm, own_ref = refs[:5]
     refs = refs[5:]
     col_ref = refs.pop(0) if rg > 1 else None
     diag_ref, dens_ref, dout_ref = refs[:3]
-    (lall, gram, wfull, wrecv, wacc, wpole, wsum, wz, tbuf, trecv, tacc, tz, tsum, tpole,
+    (inv_ref, inv_sem, far, far_gram, ss_far, rs_far, lall, gram, wfull, wrecv, wacc, wpole, wsum, wz, tbuf, trecv, tacc, tz, tsum, tpole,
      ss_z, ss_p, rs_z, rs_p, ss_wp, rs_wp, ss_wq, rs_wq, ss_wz, rs_wz,
      ss_tp, rs_tp, ss_tz, rs_tz, ss_tq, rs_tq) = refs[3:]
 
@@ -61,6 +63,17 @@
     barrier = pltpu.get_barrier_semaphore()
     for peer in peers:
         pl.semaphore_signal(barrier, inc=1, device_id=peer, device_id_type=MESH)
+    inv_copy = pltpu.make_async_copy(inv_hbm, inv_ref, inv_sem.at[0])
+    inv_copy.start()
+    here_rows = pl.ds(pl.multiple_of(rank * width, width), width)
+    for p in range(local):
+        for t in range(2):
+            for k in range(sn):
+                at = slice((t * sn + k) * width, (t * sn + k + 1) * width)
+                value = own_ref[p, :, at]
+                if lean:
+                    value = (value.astype(F32) * mask_ref[0, k].astype(F32)).astype(BF16)
+                lall[p, here_rows, at] = value
     pl.semaphore_wait(barrier, len(peers))
 
     def slot(p, chip, which):
@@ -80,16 +93,29 @@
         for sgn in (1, -1):
             @pl.when(inside(z + sgn))
             def _():
-                to_chip(own_ref.at[p], p, z, sgn, 0).start()
+                to_chip(slot(p, z, core), p, z, sgn, 0).start()
     for p in range(local):
-        to_partner(own_ref.at[p], p, z).start()
+        to_partner(slot(p, z, core), p, z).start()
+    inv_copy.wait()
+
+    def far_copy(p, chip):
+        to, rows = (1, half * 2 * width) if chip == 0 else (CHIPS - 2, 0)
+        return remote(inv_ref.at[p, pl.ds(rows, half * 2 * width)], far.at[p], ss_far.at[p], rs_far.at[p],
+                      device(to, core, q))
+
+    if lean:
+        for chip in (0, CHIPS - 1):
+            @pl.when(z == chip)
+            def _():
+                for p in range(local):
+                    far_copy(p, chip).start()
 
     poles = [order_ref[q * local + p] for p in range(local)]
-    w_re = [weight_ref[poles[p], 0] for p in range(local)]
-    w_im = [weight_ref[poles[p], 1] for p in range(local)]
+    w_re = [weight_ref[0, poles[p]] for p in range(local)]
+    w_im = [weight_ref[1, poles[p]] for p in range(local)]
 
     def column(p, a):
-        return own_ref.at[p] if rg == 1 else col_ref.at[p, a]
+        return slot(p, z, core) if lean else col_ref.at[p, a]
 
     def part_copy(t):
         return remote(wfull.at[t, :, other], wrecv.at[t], ss_wp.at[t], rs_wp.at[t], partner)
@@ -113,20 +139,30 @@
         wfull[t] = total.reshape(CHIPS, 2, width, cw)
         part_copy(t).start()
 
-    for p in range(local):
-        lall[p, pl.ds(pl.multiple_of(rank * width, width), width)] = own_ref[p]
+    def middle(chip):
+        return jnp.logical_and(chip >= 1, chip < CHIPS - 1)
+
+    def takes(chip, h):
+        if lean and h > 1:
+            return jnp.logical_and(inside(chip), middle(z)) if h == 2 else False
+        return inside(chip)
+
+    def passes_on(sgn, h):
+        if lean:
+            return middle(z + sgn) if h == 1 else False
+        return inside(z + sgn) if h < CHIPS - 1 else False
 
     def hop(h):
         for p in range(local):
             for sgn in (1, -1):
                 chip = z - sgn * h
 
-                @pl.when(inside(chip))
+                @pl.when(takes(chip, h))
                 def _():
                     here = slot(p, chip, core)
                     remote(here, here, ss_p.at[chip, p], rs_z.at[chip, p], partner).wait_recv()
-                    if h < CHIPS - 1:
-                        @pl.when(inside(z + sgn))
+                    if passes_on(sgn, h) is not False:
+                        @pl.when(passes_on(sgn, h))
                         def _():
                             to_chip(here, p, chip, sgn, h).start()
                     to_partner(here, p, chip).start()
@@ -145,7 +181,7 @@
         for sgn in (1, -1):
             chip = z - sgn * h
 
-            @pl.when(inside(chip))
+            @pl.when(takes(chip, h))
             def _():
                 accumulate(chip, False)
 
@@ -173,32 +209,54 @@
     for o in range(1, CHIPS):
         line_copy(wsum, wz, ss_wz, rs_wz, o).start()
     gather(2)
-    hop(3)
-    gather(3)
+    if not lean:
+        hop(3)
+        gather(3)
+    else:
+        for near in (1, CHIPS - 2):
+            @pl.when(z == near)
+            def _():
+                end, base = (0, half) if near == 1 else (CHIPS - 1, 0)
+                rows = pl.ds(base * 2 * width, half * 2 * width)
+                for p in range(local):
+                    far_copy(p, end).wait_recv()
+                    far_gram[p] = dot00(far[p], lall[p, rows, :])
 
     per_width = width // piece
+
+    def add_traces(traces, p, upper, lower, block):
+        m_re = upper[:, :span] - lower[:, span:]
+        m_im = lower[:, :span] + upper[:, span:]
+        n_re = w_re[p] * m_re - w_im[p] * m_im
+        n_im = w_re[p] * m_im + w_im[p] * m_re
+        both = jnp.concatenate([n_re, -n_im], axis=0)
+        high = both.astype(BF16)
+        low = (both - high.astype(F32)).astype(BF16)
+        for k in range(sn):
+            at = slice(k * width, (k + 1) * width)
+            right = jnp.concatenate([block[:, at], block[:, span + k * width:span + (k + 1) * width]], axis=0)
+            term = dot00(high[:, at], right) + dot00(low[:, at], right)
+            traces[k] = term if traces[k] is None else traces[k] + term
+
     traces = [None] * sn
     for p in range(local):
         for a in range(rg):
             base = 2 * width * a
-            upper = gram[p, base:base + width, :]
-            lower = gram[p, base + width:base + 2 * width, :]
-            m_re = upper[:, :span] - lower[:, span:]
-            m_im = lower[:, :span] + upper[:, span:]
-            n_re = w_re[p] * m_re - w_im[p] * m_im
-            n_im = w_re[p] * m_im + w_im[p] * m_re
-            both = jnp.concatenate([n_re, -n_im], axis=0)
-            high = both.astype(BF16)
-            low = (both - high.astype(F32)).astype(BF16)
-            block = column(p, a)
-            for k in range(sn):
-                at = slice(k * width, (k + 1) * width)
-                right = jnp.concatenate([block[:, at], block[:, span + k * width:span + (k + 1) * width]], axis=0)
-                term = dot00(high[:, at], right) + dot00(low[:, at], right)
-                traces[k] = term if traces[k] is None else traces[k] + term
+            add_traces(traces, p, gram[p, base:base + width, :], gram[p, base + width:base + 2 * width, :],
+                       column(p, a))
     for g in range(PC * rg):
         k, off = g // per_width, g % per_width * piece
         tbuf[g % PC // 2, g % 2, g // PC] = traces[k][off:off + piece]
+    if lean:
+        @pl.when(middle(z))
+        def _():
+            more = [None] * sn
+            for p in range(local):
+                add_traces(more, p, far_gram[p, :width, :], far_gram[p, width:, :],
+                           slot(p, (z - 1) * (CHIPS - 1), core))
+            for g in range(PC):
+                k, off = g // per_width, g % per_width * piece
+                tbuf[g // 2, g % 2, 0] += more[k][off:off + piece]
     trace_copy = remote(tbuf.at[:, other], trecv, ss_tp.at[0], rs_tp.at[0], partner)
     trace_copy.start()
 
@@ -234,30 +292,37 @@
             last_copy(o).wait_recv()
         summed = summed + functools.reduce(lambda x, y: x + y, [tpole[o] for o in range(n - 1)])
         narrow = width // n
-        result = jnp.zeros((piece, narrow), F32)
+        summed = summed.T
+        result = jnp.zeros((narrow, piece), F32)
         for t in range(n):
-            result = jnp.where(q == t, summed[:, t * narrow:(t + 1) * narrow], result)
+            result = jnp.where(q == t, summed[t * narrow:(t + 1) * narrow], result)
         dout_ref[...] = result
         for o in range(1, n):
             last_copy(o).wait_send()
 
     for p in range(local):
-        to_partner(own_ref.at[p], p, z).wait_send()
+        to_partner(slot(p, z, core), p, z).wait_send()
         for sgn in (1, -1):
             @pl.when(inside(z + sgn))
             def _():
-                to_chip(own_ref.at[p], p, z, sgn, 0).wait_send()
-            for h in range(1, CHIPS):
+                to_chip(slot(p, z, core), p, z, sgn, 0).wait_send()
+            for h in range(1, half + 1 if lean else CHIPS):
                 chip = z - sgn * h
 
-                @pl.when(inside(chip))
+                @pl.when(takes(chip, h))
                 def _():
                     here = slot(p, chip, core)
-                    if h < CHIPS - 1:
-                        @pl.when(inside(z + sgn))
+                    if passes_on(sgn, h) is not False:
+                        @pl.when(passes_on(sgn, h))
                         def _():
                             to_chip(here, p, chip, sgn, h).wait_send()
                     to_partner(here, p, chip).wait_send()
+    if lean:
+        for chip in (0, CHIPS - 1):
+            @pl.when(z == chip)
+            def _():
+                for p in range(local):
+                    far_copy(p, chip).wait_send()
     for t in range(n):
         part_copy(t).wait_send()
     for o in range(1, n):
@@ -278,22 +343,26 @@
     piece = span // (PC * rg)
     me = lax.axis_index("blk")
     mask_row = jnp.broadcast_to(ancestor_mask[0].astype(BF16)[None, :, None], (2, sn, width)).reshape(2 * span)
-    own_panel = panel_blocks * mask_row[None, None, :]
-    arrays = [pole_weights, pole_order, ancestor_mask, inverse_blocks, own_panel]
+    own_panel = panel_blocks * mask_row[None, None, :] if rg > 1 else panel_blocks
+    arrays = [pole_weights.T, pole_order, ancestor_mask, inverse_blocks, own_panel]
     if rg > 1:
         pieces = [own_panel] + [from_behind(own_panel, "blk", o * PC) for o in range(1, rg)]
         arrays.append(jnp.roll(jnp.stack(pieces[::-1], axis=1), me // PC + 1, axis=1))
     arrays.append(diag_inverse)
     smem = pl.BlockSpec(memory_space=pltpu.SMEM)
     vmem = pl.BlockSpec(memory_space=pltpu.VMEM)
-    diag_shape = (piece, width // n) if rg == 1 else (rg * piece, width)
+    diag_shape = (width // n, piece) if rg == 1 else (rg * piece, width)
     dma = pltpu.SemaphoreType.DMA
     density, diag = pl.pallas_call(
         functools.partial(kernel, (n, rg, local, width, sn)),
         out_shape=(jax.ShapeDtypeStruct((width, cw), F32), jax.ShapeDtypeStruct(diag_shape, F32)),
-        in_specs=[smem] * 3 + [vmem] * (len(arrays) - 3),
+        in_specs=[smem] * 3 + [pl.BlockSpec(memory_space=pl.ANY)] + [vmem] * (len(arrays) - 4),
         out_specs=(vmem, vmem),
         scratch_shapes=[
+            pltpu.VMEM(inverse_blocks.shape, BF16), dma((1,)),
+            pltpu.VMEM((local, CHIPS // 2 * 2 * width, 2 * width) if rg == 1 else (8, 128), BF16),
+            pltpu.VMEM((local, 2 * width, 2 * span) if rg == 1 else (8, 128), F32),
+            dma((local,)), dma((local,)),
             pltpu.VMEM((local, PC * width, 2 * span), BF16),
             pltpu.VMEM((local, rg * 2 * width, 2 * span), F32),
             pltpu.VMEM((n, CHIPS, 2, width, cw), F32),
@@ -323,6 +392,8 @@
             pairs[:, 0, None, None] * diag_inverse[..., :width] - pairs[:, 1, None, None] * diag_inverse[..., width:],
             axis=0)
         diag = lax.psum_scatter(diag, "pole", scatter_dimension=1, tiled=True)
+    else:
+        diag = diag.T
     return density, diag
 
 

time: 66.2 us -> 50.1 us (0.76)
  Pallas kernels: 58.4 us -> 47.2 us
  other arithmetic: 2.52 us -> 0 us
  local copies, waits for them, and re-layouts: 4.33 us -> 2.09 us
    pallas_call x1, Pallas kernels: 58.4 us -> 47.2 us  [per_device(): pl.pallas_call(functools.partial(kernel, (n, rg, local, width, sn)), out_...]
    mul x1 -> x0, other arithmetic: 1.86 us -> none  [per_device(): own_panel = panel_blocks * mask_row[None, None, :]]
    pallas_call x1 -> x0, local copies, waits for them, and re-layouts: 1.44 us -> none  [per_device(): pl.pallas_call(functools.partial(kernel, (n, rg, local, width, sn)), out_...]
    unnamed x4, local copies, waits for them, and re-layouts: 2.82 us -> 2.09 us
where the time goes in v2:
time: 50.1 us; the launch traced here: 49.9 us
  Pallas kernels  47.2 us (94%)
  local copies, waits for them, and re-layouts  2.09 us (4%)
  between operations  0.65 us (1%)
    pallas_call x1, Pallas kernels, per_device(): pl.pallas_call(functools.partial(kernel, (n, rg, local, width, sn)), out_...  47.2 us
    unnamed x4, local copies, waits for them, and re-layouts  2.09 us

profile of v2, /device:TPU:0, one launch (start us, length us, event | category | flops | bytes accessed | tf_op | source)
XLA Modules:
  0.0 49.9 jit_solution(2556232595282356704)
XLA Ops:
  0.6 47.2 %shard_map.77 = (f32[128,128]{1,0:T(8,128)}, f32[32,64]{1,0:T(8,128)}) custom-call(f32[2,8]{1,0:T(2,128)} %bitcast.3, s32[8]{0:T(128)} %refs_1_.1, s32[1,4]{1,0:T(1,128)} %refs_2_.1, bf16[2,1024,256]{2,1,0:T(8,128)(2,1)} %refs_3_.1, bf16[2,128,1024]{2,1,0:T(8,128)(2,1)} %refs_4_.1, f32[2,64,256]{2,1,0:T(8,128)} %refs_5_.1), custom_call_target="tpu_custom_call" | custom-call | tf_op jit(solution)/shard_map/pallas_call | solution.py:356
  47.8 0.0 copy-start
  47.8 1.5 %copy.10 = f32[128,128]{1,0:T(8,128)} copy(f32[128,128]{1,0:T(8,128)} %get-tuple-element.8) | data formatting | bytes 131072
  49.3 0.0 copy-done
  49.3 0.6 %copy.11 = f32[64,32]{0,1:T(8,128)} copy(f32[64,32]{0,1:T(8,128)S(1)} %bitcast.2) | data formatting | bytes 16384
Async XLA Ops:
  47.8 1.5 %copy-start = (f32[32,64]{1,0:T(8,128)S(1)}, f32[32,64]{1,0:T(8,128)}, u32[]{:S(2)}) copy-start(f32[32,64]{1,0:T(8,128)} %get-tuple-element.5) | copy-start | bytes 24580

commit v3 on v2

--- a/solution.py
+++ b/solution.py
@@ -35,7 +35,7 @@
     refs = refs[5:]
     col_ref = refs.pop(0) if rg > 1 else None
     diag_ref, dens_ref, dout_ref = refs[:3]
-    (inv_ref, inv_sem, far, far_gram, ss_far, rs_far, lall, gram, wfull, wrecv, wacc, wpole, wsum, wz, tbuf, trecv, tacc, tz, tsum, tpole,
+    (inv_ref, inv_sem, far, far_gram, tt, ss_far, rs_far, lall, gram, wfull, wrecv, wacc, wpole, wsum, wz, tbuf, trecv, tacc, tz, tsum, tpole,
      ss_z, ss_p, rs_z, rs_p, ss_wp, rs_wp, ss_wq, rs_wq, ss_wz, rs_wz,
      ss_tp, rs_tp, ss_tz, rs_tz, ss_tq, rs_tq) = refs[3:]
 
@@ -152,8 +152,10 @@
             return middle(z + sgn) if h == 1 else False
         return inside(z + sgn) if h < CHIPS - 1 else False
 
-    def hop(h):
-        for p in range(local):
+    every = range(local)
+
+    def hop(h, ps=every):
+        for p in ps:
             for sgn in (1, -1):
                 chip = z - sgn * h
 
@@ -167,9 +169,9 @@
                             to_chip(here, p, chip, sgn, h).start()
                     to_partner(here, p, chip).start()
 
-    def accumulate(chip, fresh):
+    def accumulate(chip, fresh, ps=every):
         rows = pl.ds(pl.multiple_of(chip * 2 * width, 2 * width), 2 * width)
-        for p in range(local):
+        for p in ps:
             theirs = slot(p, chip, other)
             remote(theirs, theirs, ss_p.at[chip, p], rs_p.at[chip, p], partner).wait_recv()
             for a in range(rg):
@@ -177,13 +179,13 @@
                 term = dot00(inv_ref[p, rows, at], lall[p, rows, :])
                 gram[p, at, :] = term if fresh else gram[p, at, :] + term
 
-    def gather(h):
+    def gather(h, ps=every):
         for sgn in (1, -1):
             chip = z - sgn * h
 
             @pl.when(takes(chip, h))
             def _():
-                accumulate(chip, False)
+                accumulate(chip, False, ps)
 
     def pole_copy(o):
         to = lax.rem(q + o, n)
@@ -202,29 +204,10 @@
             pole_copy(o).start()
     accumulate(z, True)
     gather(1)
-    hop(2)
-    for o in range(1, n):
-        pole_copy(o).wait_recv()
-    wsum[...] = wacc[q] + functools.reduce(lambda x, y: x + y, [wpole[o] for o in range(n - 1)])
-    for o in range(1, CHIPS):
-        line_copy(wsum, wz, ss_wz, rs_wz, o).start()
-    gather(2)
-    if not lean:
-        hop(3)
-        gather(3)
-    else:
-        for near in (1, CHIPS - 2):
-            @pl.when(z == near)
-            def _():
-                end, base = (0, half) if near == 1 else (CHIPS - 1, 0)
-                rows = pl.ds(base * 2 * width, half * 2 * width)
-                for p in range(local):
-                    far_copy(p, end).wait_recv()
-                    far_gram[p] = dot00(far[p], lall[p, rows, :])
 
     per_width = width // piece
 
-    def add_traces(traces, p, upper, lower, block):
+    def add_traces(fresh, p, upper, lower, block):
         m_re = upper[:, :span] - lower[:, span:]
         m_im = lower[:, :span] + upper[:, span:]
         n_re = w_re[p] * m_re - w_im[p] * m_im
@@ -234,29 +217,52 @@
         low = (both - high.astype(F32)).astype(BF16)
         for k in range(sn):
             at = slice(k * width, (k + 1) * width)
-            right = jnp.concatenate([block[:, at], block[:, span + k * width:span + (k + 1) * width]], axis=0)
-            term = dot00(high[:, at], right) + dot00(low[:, at], right)
-            traces[k] = term if traces[k] is None else traces[k] + term
-
-    traces = [None] * sn
-    for p in range(local):
+            left = jnp.concatenate([block[:, at], block[:, span + k * width:span + (k + 1) * width]], axis=0)
+            term = dot00(left, jnp.concatenate([high[:, at], low[:, at]], axis=1))
+            term = term[:, :width] + term[:, width:]
+            tt[k] = term if fresh else tt[k] + term
+
+    def own_traces(p):
         for a in range(rg):
             base = 2 * width * a
-            add_traces(traces, p, gram[p, base:base + width, :], gram[p, base + width:base + 2 * width, :],
-                       column(p, a))
-    for g in range(PC * rg):
-        k, off = g // per_width, g % per_width * piece
-        tbuf[g % PC // 2, g % 2, g // PC] = traces[k][off:off + piece]
+            add_traces(p == 0 and a == 0, p, gram[p, base:base + width, :],
+                       gram[p, base + width:base + 2 * width, :], column(p, a))
+
+    def reduce_density():
+        for o in range(1, n):
+            pole_copy(o).wait_recv()
+        wsum[...] = wacc[q] + functools.reduce(lambda x, y: x + y, [wpole[o] for o in range(n - 1)])
+        for o in range(1, CHIPS):
+            line_copy(wsum, wz, ss_wz, rs_wz, o).start()
+
     if lean:
-        @pl.when(middle(z))
-        def _():
-            more = [None] * sn
-            for p in range(local):
-                add_traces(more, p, far_gram[p, :width, :], far_gram[p, width:, :],
-                           slot(p, (z - 1) * (CHIPS - 1), core))
-            for g in range(PC):
-                k, off = g // per_width, g % per_width * piece
-                tbuf[g // 2, g % 2, 0] += more[k][off:off + piece]
+        for p in range(local):
+            hop(2, [p])
+            gather(2, [p])
+            own_traces(p)
+            for near in (1, CHIPS - 2):
+                @pl.when(z == near)
+                def _():
+                    end, base = (0, half) if near == 1 else (CHIPS - 1, 0)
+                    rows = slice(base * 2 * width, (base + half) * 2 * width)
+                    far_copy(p, end).wait_recv()
+                    far_gram[p] = dot00(far[p], lall[p, rows, :])
+                    add_traces(False, p, far_gram[p, :width, :], far_gram[p, width:, :], slot(p, end, core))
+            if p == 0:
+                reduce_density()
+    else:
+        hop(2)
+        reduce_density()
+        gather(2)
+        hop(3)
+        gather(3)
+        for p in range(local):
+            own_traces(p)
+    for k in range(sn):
+        trace = tt[k].T
+        for g in range(k * per_width, (k + 1) * per_width):
+            off = g % per_width * piece
+            tbuf[g % PC // 2, g % 2, g // PC] = trace[off:off + piece]
     trace_copy = remote(tbuf.at[:, other], trecv, ss_tp.at[0], rs_tp.at[0], partner)
     trace_copy.start()
 
@@ -280,23 +286,20 @@
         summed = summed.reshape(piece, width)
         for p in range(local):
             summed = summed + w_re[p] * diag_ref[p, :, :width] - w_im[p] * diag_ref[p, :, width:]
-        tsum[...] = summed
+        narrow = width // n
+        summed = summed.T
+        for t in range(n):
+            tsum[t] = summed[t * narrow:(t + 1) * narrow]
 
         def last_copy(o):
-            return remote(tsum, tpole.at[o - 1], ss_tq.at[o - 1], rs_tq.at[o - 1],
-                          device(z, core, lax.rem(q + o, n)))
+            to = lax.rem(q + o, n)
+            return remote(tsum.at[to], tpole.at[o - 1], ss_tq.at[o - 1], rs_tq.at[o - 1], device(z, core, to))
 
         for o in range(1, n):
             last_copy(o).start()
         for o in range(1, n):
             last_copy(o).wait_recv()
-        summed = summed + functools.reduce(lambda x, y: x + y, [tpole[o] for o in range(n - 1)])
-        narrow = width // n
-        summed = summed.T
-        result = jnp.zeros((narrow, piece), F32)
-        for t in range(n):
-            result = jnp.where(q == t, summed[t * narrow:(t + 1) * narrow], result)
-        dout_ref[...] = result
+        dout_ref[...] = tsum[q] + functools.reduce(lambda x, y: x + y, [tpole[o] for o in range(n - 1)])
         for o in range(1, n):
             last_copy(o).wait_send()
 
@@ -331,6 +334,14 @@
     for o in range(1, CHIPS):
         line_copy(wsum, wz, ss_wz, rs_wz, o).wait_send()
         line_copy(tacc, tz, ss_tz, rs_tz, o).wait_send()
+
+
+def land(*arrays):
+    def move(*refs):
+        for source, target in zip(refs[:len(arrays)], refs[len(arrays):]):
+            target[...] = source[...]
+
+    return pl.pallas_call(move, out_shape=[jax.ShapeDtypeStruct(x.shape, x.dtype) for x in arrays])(*arrays)
 
 
 def per_device(inverse_blocks, panel_blocks, ancestor_mask, diag_inverse, pole_weights, pole_order):
@@ -362,6 +373,7 @@
             pltpu.VMEM(inverse_blocks.shape, BF16), dma((1,)),
             pltpu.VMEM((local, CHIPS // 2 * 2 * width, 2 * width) if rg == 1 else (8, 128), BF16),
             pltpu.VMEM((local, 2 * width, 2 * span) if rg == 1 else (8, 128), F32),
+            pltpu.VMEM((sn, width, width), F32),
             dma((local,)), dma((local,)),
             pltpu.VMEM((local, PC * width, 2 * span), BF16),
             pltpu.VMEM((local, rg * 2 * width, 2 * span), F32),
@@ -375,8 +387,8 @@
             pltpu.VMEM((CHIPS, rg, piece, width), F32),
             pltpu.VMEM((CHIPS, rg, piece, width), F32),
             pltpu.VMEM((CHIPS - 1, rg, piece, width), F32),
-            pltpu.VMEM((piece, width), F32),
-            pltpu.VMEM((n - 1, piece, width), F32),
+            pltpu.VMEM((n, width // n, piece), F32),
+            pltpu.VMEM((n - 1, width // n, piece), F32),
             dma((2, CHIPS - 1, local)), dma((CHIPS, local)), dma((CHIPS, local)), dma((CHIPS, local)),
             dma((n,)), dma((n,)), dma((n - 1,)), dma((n - 1,)), dma((CHIPS - 1,)), dma((CHIPS - 1,)),
             dma((1,)), dma((1,)), dma((CHIPS - 1,)), dma((CHIPS - 1,)), dma((n - 1,)), dma((n - 1,)),
@@ -393,6 +405,7 @@
             axis=0)
         diag = lax.psum_scatter(diag, "pole", scatter_dimension=1, tiled=True)
     else:
+        density, diag = land(density, diag)
         diag = diag.T
     return density, diag
 

time: 50.1 us -> 49.4 us (0.986)
  local copies, waits for them, and re-layouts: 2.09 us -> 0 us
  Pallas kernels: 47.2 us -> 48.6 us
    unnamed x4 -> x0, local copies, waits for them, and re-layouts: 2.09 us -> none
    pallas_call x0 -> x1, Pallas kernels: none -> 1.48 us  [land(): pl.pallas_call(move, out_shape=[jax.ShapeDtypeStruct(x.shape, x.dtype) fo...]
where the time goes in v3:
time: 49.4 us; the launch traced here: 49.2 us
  Pallas kernels  48.6 us (98%)
  between operations  0.64 us (1%)
    pallas_call x1, Pallas kernels, per_device(): pl.pallas_call(functools.partial(kernel, (n, rg, local, width, sn)), out_...  47.1 us
    pallas_call x1, Pallas kernels, land(): pl.pallas_call(move, out_shape=[jax.ShapeDtypeStruct(x.shape, x.dtype) fo...  1.48 us

profile of v3, /device:TPU:0, one launch (start us, length us, event | category | flops | bytes accessed | tf_op | source)
XLA Modules:
  0.0 49.2 jit_solution(12945836258375627585)
XLA Ops:
  0.6 47.1 %shard_map.77 = (f32[128,128]{1,0:T(8,128)}, f32[32,64]{1,0:T(8,128)}) custom-call(f32[2,8]{1,0:T(2,128)} %bitcast.2, s32[8]{0:T(128)} %refs_1_.1, s32[1,4]{1,0:T(1,128)} %refs_2_.1, bf16[2,1024,256]{2,1,0:T(8,128)(2,1)} %refs_3_.1, bf16[2,128,1024]{2,1,0:T(8,128)(2,1)} %refs_4_.1, f32[2,64,256]{2,1,0:T(8,128)} %refs_5_.1), custom_call_target="tpu_custom_call" | custom-call | tf_op jit(solution)/shard_map/pallas_call | solution.py:367
  47.7 1.5 %shard_map.78 = (f32[128,128]{1,0:T(8,128)}, f32[32,64]{1,0:T(8,128)}) custom-call(f32[128,128]{1,0:T(8,128)} %get-tuple-element.6.refs_0_, f32[32,64]{1,0:T(8,128)} %get-tuple-element.7.refs_1_), custom_call_target="tpu_custom_call" | custom-call | tf_op jit(solution)/shard_map/pallas_call | solution.py:344

commit v4 on v3

--- a/solution.py
+++ b/solution.py
@@ -120,8 +120,20 @@
     def part_copy(t):
         return remote(wfull.at[t, :, other], wrecv.at[t], ss_wp.at[t], rs_wp.at[t], partner)
 
-    order = [lax.rem(q + o, n) for o in list(range(1, n)) + [0]]
-    for t in order:
+    def pole_copy(o):
+        to = lax.rem(q + o, n)
+        return remote(wacc.at[to], wpole.at[o - 1], ss_wq.at[o - 1], rs_wq.at[o - 1], device(z, core, to))
+
+    def join_cores(o):
+        t = lax.rem(q + o, n)
+        part_copy(t).wait_recv()
+        wacc[t] = wfull[t, :, core] + wrecv[t]
+        if o:
+            pole_copy(o).start()
+
+    shifts = list(range(1, n)) + [0]
+    for place, o in enumerate(shifts):
+        t = lax.rem(q + o, n)
         total = None
         for p in range(local):
             product = None
@@ -138,6 +150,8 @@
             total = term if total is None else total + term
         wfull[t] = total.reshape(CHIPS, 2, width, cw)
         part_copy(t).start()
+        if place:
+            join_cores(shifts[place - 1])
 
     def middle(chip):
         return jnp.logical_and(chip >= 1, chip < CHIPS - 1)
@@ -187,21 +201,12 @@
             def _():
                 accumulate(chip, False, ps)
 
-    def pole_copy(o):
-        to = lax.rem(q + o, n)
-        return remote(wacc.at[to], wpole.at[o - 1], ss_wq.at[o - 1], rs_wq.at[o - 1], device(z, core, to))
-
     def line_copy(src, dst, send, recv, o):
         to = lax.rem(z + o, CHIPS)
         return remote(src.at[to], dst.at[o - 1], send.at[o - 1], recv.at[o - 1], device(to, core, q))
 
     hop(1)
-    for o in list(range(1, n)) + [0]:
-        t = lax.rem(q + o, n)
-        part_copy(t).wait_recv()
-        wacc[t] = wfull[t, :, core] + wrecv[t]
-        if o:
-            pole_copy(o).start()
+    join_cores(0)
     accumulate(z, True)
     gather(1)
 

time: 49.4 us -> 47.9 us (0.970)
  Pallas kernels: 48.6 us -> 47 us
    pallas_call x1, Pallas kernels: 47.1 us -> 45.6 us  [per_device(): pl.pallas_call(functools.partial(kernel, (n, rg, local, width, sn)), out_...]
where the time goes in v4:
time: 47.9 us; the launch traced here: 47.7 us
  Pallas kernels  47 us (98%)
  between operations  0.64 us (1%)
    pallas_call x1, Pallas kernels, per_device(): pl.pallas_call(functools.partial(kernel, (n, rg, local, width, sn)), out_...  45.6 us
    pallas_call x1, Pallas kernels, land(): pl.pallas_call(move, out_shape=[jax.ShapeDtypeStruct(x.shape, x.dtype) fo...  1.48 us

profile of v4, /device:TPU:0, one launch (start us, length us, event | category | flops | bytes accessed | tf_op | source)
XLA Modules:
  0.0 47.7 jit_solution(14885250949912354522)
XLA Ops:
  0.6 45.6 %shard_map.77 = (f32[128,128]{1,0:T(8,128)}, f32[32,64]{1,0:T(8,128)}) custom-call(f32[2,8]{1,0:T(2,128)} %bitcast.2, s32[8]{0:T(128)} %refs_1_.1, s32[1,4]{1,0:T(1,128)} %refs_2_.1, bf16[2,1024,256]{2,1,0:T(8,128)(2,1)} %refs_3_.1, bf16[2,128,1024]{2,1,0:T(8,128)(2,1)} %refs_4_.1, f32[2,64,256]{2,1,0:T(8,128)} %refs_5_.1), custom_call_target="tpu_custom_call" | custom-call | tf_op jit(solution)/shard_map/pallas_call | solution.py:372
  46.2 1.5 %shard_map.78 = (f32[128,128]{1,0:T(8,128)}, f32[32,64]{1,0:T(8,128)}) custom-call(f32[128,128]{1,0:T(8,128)} %get-tuple-element.6.refs_0_, f32[32,64]{1,0:T(8,128)} %get-tuple-element.7.refs_1_), custom_call_target="tpu_custom_call" | custom-call | tf_op jit(solution)/shard_map/pallas_call | solution.py:349
